TPU v7x, 32 devices: a whole 2x2x4 slice. The times are simulated.
32 devices in a mesh: row: 8 (over z, core), col: 4 (over y, x).
Axes of the slice: x: 2, y: 2, z: 4, core: 2. Of those that a mesh axis runs over, the one named last changes fastest.
Arguments:
- factor: float32 [10240, 10240], P('row', 'col'), may hold values from -1 to 6, as said below
Outputs:
- progressed: float32 [10240, 10240], P('row', 'col')
Inputs may be any that keep to these rules, and one draw needn't show every extreme that they name: factor is symmetric positive definite with smallest eigenvalue at least 0.5, stored in the block-cyclic order of the steps.
All inputs are finite; a program needn't handle non-finite values.
Results may differ from a plain program's by a relative error of at most 0.0001.
Values sent between devices are 32-bit elements; how exact they have to be, the bound alone decides.
A program may use at most 128 MiB of HBM per device.

v0:
```python
import jax
import jax.numpy as jnp
from jax import lax
from jax.sharding import PartitionSpec as P

TILE = 128
PIVOT = 512
STEPS = 2


def broadcast(value, axis, source):
    kept = jnp.where(lax.axis_index(axis) == source, value, 0).astype(value.dtype)
    return lax.psum(kept, axis)


def per_device(factor):
    rows_count = lax.axis_size("row")
    cols_count = lax.axis_size("col")
    local_rows, local_cols = factor.shape
    row_place = lax.axis_index("row")
    col_place = lax.axis_index("col")
    per_block = PIVOT // TILE
    row_offsets = jnp.arange(local_rows, dtype=jnp.int32)
    row_global = (row_offsets // TILE * rows_count + row_place) * TILE + row_offsets % TILE
    pivot_range = jnp.arange(PIVOT, dtype=jnp.int32)
    identity = jnp.eye(PIVOT, dtype=jnp.float32)

    def gather_columns(slab_of, step):
        slabs = []
        for member in range(per_block):
            tile_no = step * per_block + member
            slabs.append(broadcast(slab_of(tile_no), "col", tile_no % cols_count))
        return jnp.concatenate(slabs, axis=1)

    def plain_slab(matrix):

        def taker(tile_no):
            first = tile_no // cols_count * TILE
            return matrix[:, first : first + TILE]

        return taker

    matrix = factor
    column_panel = gather_columns(plain_slab(matrix), 0)
    for step in range(STEPS):
        row_parts = []
        block_parts = []
        for prepare_member in range(per_block):
            prepare_tile_no = step * per_block + prepare_member
            prepare_first = prepare_tile_no // rows_count * TILE
            got_rows, got_block = (
                broadcast(
                    matrix[prepare_first : prepare_first + TILE, :],
                    "row",
                    prepare_tile_no % rows_count,
                ),
                broadcast(
                    column_panel[prepare_first : prepare_first + TILE, :],
                    "row",
                    prepare_tile_no % rows_count,
                ),
            )
            row_parts.append(got_rows)
            block_parts.append(got_block)
        pivot_rows = jnp.concatenate(row_parts, axis=0)
        pivot_block = jnp.concatenate(block_parts, axis=0)
        lower = jnp.linalg.cholesky(pivot_block)
        prepare_inverse = jax.scipy.linalg.cho_solve((lower, True), identity)
        prepare_scaled = jnp.dot(
            prepare_inverse,
            pivot_rows,
            precision=lax.Precision.HIGHEST,
            preferred_element_type=jnp.float32,
        )
        prepare_marks = (row_global[:, None] - step * PIVOT == pivot_range[None, :]).astype(
            jnp.float32
        )
        prepare_reduced = column_panel - prepare_marks
        prepared = (prepare_inverse, prepare_scaled, prepare_marks, prepare_reduced)
        if step + 1 < STEPS:
            scaled_now = prepared[1]
            reduced_now = prepared[3]

            def early_slab(tile_no, source=matrix, scaled_now=scaled_now, reduced_now=reduced_now):
                first = tile_no // cols_count * TILE
                return source[:, first : first + TILE] - jnp.dot(
                    reduced_now,
                    scaled_now[:, first : first + TILE],
                    precision=lax.Precision.HIGHEST,
                    preferred_element_type=jnp.float32,
                )

            next_panel = gather_columns(early_slab, step + 1)
        inverse, scaled, marks, reduced = prepared
        updated = matrix - jnp.dot(
            reduced, scaled, precision=lax.Precision.HIGHEST, preferred_element_type=jnp.float32
        )
        fixed = marks - jnp.dot(
            reduced, inverse, precision=lax.Precision.HIGHEST, preferred_element_type=jnp.float32
        )
        for finish_member in range(per_block):
            finish_tile_no = step * per_block + finish_member
            finish_first = finish_tile_no // cols_count * TILE
            current = updated[:, finish_first : finish_first + TILE]
            chosen = jnp.where(
                col_place == finish_tile_no % cols_count,
                fixed[:, finish_member * TILE : (finish_member + 1) * TILE],
                current,
            )
            updated = updated.at[:, finish_first : finish_first + TILE].set(chosen)
        matrix = updated
        if step + 1 < STEPS:
            column_panel = next_panel
    return matrix


def solution(mesh):
    placed = (P("row", "col"),)
    return jax.shard_map(
        per_device, mesh=mesh, in_specs=placed, out_specs=P("row", "col"), check_vma=False
    )
```

profile of v0, /device:TPU:0, one launch (start us, length us, event | category | flops | bytes accessed | tf_op | source)
XLA Modules:
  0.0 923.6 jit_solution(14794230671533546266)
XLA Ops:
  6.5 13.9 %copy.5 = f32[1280,2560]{0,1:T(8,128)} copy(f32[1280,2560]{1,0:T(8,128)} %param.20) | data formatting | bytes 26214400 | tf_op args[0]
  20.4 2.6 slice_select_fusion.8
  23.1 3.8 slice_select_fusion.7
  26.9 77.3 %all-reduce.16.cloned.1.call-done = (f32[1280,128]{0,1:T(8,128)}, f32[1280,128]{0,1:T(8,128)}, f32[1280,128]{0,1:T(8,128)}, f32[1280,128]{0,1:T(8,128)}) async-done(((f32[1280,128]{0,1:T(8,128)}, f32[1280,128]{0,1:T(8,128)}, f32[1280,128]{0,1:T(8,128)}, f32[1280,128]{0,1:T(8,128)}), (f32[1280,128]{0,1:T(8,128)}, f32[1280,128]{0,1:T(8,128)}, f32[1280,128]{0,1:T(8,128)}, ...) | async-done | bytes 2621456 | tf_op jit(solution)/shard_map/psum | solution.py:13
  109.6 134.5 %all-reduce.12.cloned.1.call-done = (f32[128,2560]{0,1:T(8,128)}, f32[128,2560]{0,1:T(8,128)}, f32[128,2560]{0,1:T(8,128)}, f32[128,2560]{0,1:T(8,128)}, f32[128...) async-done(((f32[128,2560]{0,1:T(8,128)}, f32[128,2560]{0,1:T(8,128)}, f32[128,2560]{0,1:T(8,128)}, f32[128,2560]{0,1:T(8,128)}, ...) | async-done | bytes 6291472 | tf_op jit(solution)/shard_map/psum | solution.py:13
  244.1 1.7 constant_dynamic-update-slice_fusion.7
  245.8 1.7 constant_dynamic-update-slice_fusion.6
  247.5 1.7 constant_dynamic-update-slice_fusion.5
  249.2 1.7 constant_dynamic-update-slice_fusion.4
  250.9 2.6 copy.3
  253.5 1.8 fusion.22
  256.2 11.7 %cholesky.286 = f32[128,128]{1,0:T(8,128)S(1)} custom-call(f32[128,128]{1,0:T(8,128)S(1)} %cholesky.426), custom_call_target="Cholesky" | custom-call | tf_op jit(solution)/shard_map/jit(cholesky)/cholesky | solution.py:67
  268.0 9.8 %custom-call.29 = f32[1,128,128]{1,2,0:T(8,128)S(1)} custom-call(f32[1,128,128]{2,1,0:T(8,128)S(1)} %get-tuple-element.214), custom_call_target="InvertDiagBlocksLowerTriangular" | custom-call | tf_op jit(solution)/shard_map/jit(cholesky)/cholesky | solution.py:67
  278.9 1.9 constant_dynamic-update-slice_fusion.19
  282.1 11.7 %cholesky.305 = f32[128,128]{1,0:T(8,128)S(1)} custom-call(f32[128,128]{1,0:T(8,128)S(1)} %cholesky.430), custom_call_target="Cholesky" | custom-call | tf_op jit(solution)/shard_map/jit(cholesky)/cholesky | solution.py:67
  294.5 10.0 %custom-call.30 = f32[1,128,128]{1,2,0:T(8,128)S(1)} custom-call(f32[1,128,128]{2,1,0:T(8,128)S(1)} %get-tuple-element.211), custom_call_target="InvertDiagBlocksLowerTriangular" | custom-call | tf_op jit(solution)/shard_map/jit(cholesky)/cholesky | solution.py:67
  306.9 11.7 %cholesky.326 = f32[128,128]{1,0:T(8,128)S(1)} custom-call(f32[128,128]{1,0:T(8,128)S(1)} %cholesky.435), custom_call_target="Cholesky" | custom-call | tf_op jit(solution)/shard_map/jit(cholesky)/cholesky | solution.py:67
  319.9 9.8 %custom-call.31 = f32[1,128,128]{1,2,0:T(8,128)S(1)} custom-call(f32[1,128,128]{2,1,0:T(8,128)S(1)} %get-tuple-element.208), custom_call_target="InvertDiagBlocksLowerTriangular" | custom-call | tf_op jit(solution)/shard_map/jit(cholesky)/cholesky | solution.py:67
  332.0 22.1 %cholesky.343 = f32[128,128]{1,0:T(8,128)S(1)} custom-call(f32[128,128]{1,0:T(8,128)S(1)} %convolution_subtract_fusion.20), custom_call_target="Cholesky" | custom-call | tf_op jit(solution)/shard_map/jit(cholesky)/cholesky | solution.py:67
  358.5 2.3 select_select_fusion.1
  360.9 11.7 %while.12 = (s32[]{:T(128)}, f32[512,512]{1,0:T(8,128)}, s32[4,2]{0,1:T(2,128)S(1)}, f32[4,128,128]{2,1,0:T(8,128)S(1)}, s32[]{:T(128)}) while((s32[]{:T(128)}, f32[512,512]{1,0:T(8,128)}, s32[4,2]{0,1:T(2,128)S(1)}, f32[4,128,128]{2,1,0:T(8,128)S(1)}, s32[]{:T(128)}) %tuple.105), condition=%wide.while_cond.8, body=%wide.while_body.8.sunk | while | flops 2 | bytes 131189 | solution.py:68
  361.6 2.3 bitcast_dynamic-update-slice_fusion.4
  364.5 2.3 bitcast_dynamic-update-slice_fusion.4
  367.4 2.3 bitcast_dynamic-update-slice_fusion.4
  370.4 2.2 bitcast_dynamic-update-slice_fusion.4
  372.6 39.3 %custom-call.32 = f32[4,128,128]{1,2,0:T(8,128)S(1)} custom-call(f32[4,128,128]{2,1,0:T(8,128)S(1)} %get-tuple-element.117), custom_call_target="InvertDiagBlocksLowerTriangular" | custom-call | tf_op jit(solution)/shard_map/jit(_cho_solve)/triangular_solve | solution.py:68
  422.3 6.2 convert_subtract_fusion.2
  428.6 9.2 fusion
  437.8 3.6 broadcast_select_fusion
  441.5 26.3 %convolution_subtract_fusion.1 = f32[1280,2560]{0,1:T(8,128)} fusion(f32[1280,2560]{0,1:T(8,128)S(1)} %bitcast.117, f32[512,2560]{1,0:T(8,128)S(1)} %fusion, f32[1280,512]{0,1:T(8,128)S(1)} %constant_dynamic-update-slice_fusion, s32[1280]{0:T(1024)S(1)} %fusion.122), kind=kOutput, calls=%fused_computation.5 | convolution fusion | flops 20137902080 | bytes 34083840 | tf_op jit(solution)/shard_map/dot_general | solution.py:95
  467.8 1.7 copy-done
  469.4 2.6 constant_dynamic-update-slice_fusion.23
  476.6 3.8 slice_select_fusion.3
  480.3 65.9 %all-reduce.14.cloned.1.call-done = (f32[1280,128]{0,1:T(8,128)}, f32[1280,128]{0,1:T(8,128)}, f32[1280,128]{0,1:T(8,128)}, f32[1280,128]{0,1:T(8,128)}) async-done(((f32[1280,128]{0,1:T(8,128)}, f32[1280,128]{0,1:T(8,128)}, f32[1280,128]{0,1:T(8,128)}, f32[1280,128]{0,1:T(8,128)}), (f32[1280,128]{0,1:T(8,128)}, f32[1280,128]{0,1:T(8,128)}, f32[1280,128]{0,1:T(8,128)}, ...) | async-done | bytes 2621456 | tf_op jit(solution)/shard_map/psum | solution.py:13
  550.8 135.4 %all-reduce.10.cloned.1.call-done = (f32[128,2560]{0,1:T(8,128)}, f32[128,2560]{0,1:T(8,128)}, f32[128,2560]{0,1:T(8,128)}, f32[128,2560]{0,1:T(8,128)}, f32[128...) async-done(((f32[128,2560]{0,1:T(8,128)}, f32[128,2560]{0,1:T(8,128)}, f32[128,2560]{0,1:T(8,128)}, f32[128,2560]{0,1:T(8,128)}, ...) | async-done | bytes 6291472 | tf_op jit(solution)/shard_map/psum | solution.py:13
  686.2 1.7 constant_dynamic-update-slice_fusion.15
  687.9 1.7 constant_dynamic-update-slice_fusion.14
  689.6 1.7 constant_dynamic-update-slice_fusion.13
  691.3 1.7 constant_dynamic-update-slice_fusion.12
  693.0 2.5 copy.10
  695.6 1.8 fusion.21
  698.4 11.7 %cholesky.358 = f32[128,128]{1,0:T(8,128)S(1)} custom-call(f32[128,128]{1,0:T(8,128)S(1)} %cholesky.439), custom_call_target="Cholesky" | custom-call | tf_op jit(solution)/shard_map/jit(cholesky)/cholesky | solution.py:67
  710.8 9.8 %custom-call.33 = f32[1,128,128]{1,2,0:T(8,128)S(1)} custom-call(f32[1,128,128]{2,1,0:T(8,128)S(1)} %get-tuple-element.204), custom_call_target="InvertDiagBlocksLowerTriangular" | custom-call | tf_op jit(solution)/shard_map/jit(cholesky)/cholesky | solution.py:67
  721.7 1.9 constant_dynamic-update-slice_fusion.17
  724.9 11.7 %cholesky.377 = f32[128,128]{1,0:T(8,128)S(1)} custom-call(f32[128,128]{1,0:T(8,128)S(1)} %cholesky.443), custom_call_target="Cholesky" | custom-call | tf_op jit(solution)/shard_map/jit(cholesky)/cholesky | solution.py:67
  738.0 10.2 %custom-call.34 = f32[1,128,128]{1,2,0:T(8,128)S(1)} custom-call(f32[1,128,128]{2,1,0:T(8,128)S(1)} %get-tuple-element.201), custom_call_target="InvertDiagBlocksLowerTriangular" | custom-call | tf_op jit(solution)/shard_map/jit(cholesky)/cholesky | solution.py:67
  750.5 11.7 %cholesky.398 = f32[128,128]{1,0:T(8,128)S(1)} custom-call(f32[128,128]{1,0:T(8,128)S(1)} %cholesky.448), custom_call_target="Cholesky" | custom-call | tf_op jit(solution)/shard_map/jit(cholesky)/cholesky | solution.py:67
  763.5 9.8 %custom-call.35 = f32[1,128,128]{1,2,0:T(8,128)S(1)} custom-call(f32[1,128,128]{2,1,0:T(8,128)S(1)} %get-tuple-element.198), custom_call_target="InvertDiagBlocksLowerTriangular" | custom-call | tf_op jit(solution)/shard_map/jit(cholesky)/cholesky | solution.py:67
  775.6 11.9 %cholesky.415 = f32[128,128]{1,0:T(8,128)S(1)} custom-call(f32[128,128]{1,0:T(8,128)S(1)} %convolution_subtract_fusion.19), custom_call_target="Cholesky" | custom-call | tf_op jit(solution)/shard_map/jit(cholesky)/cholesky | solution.py:67
  791.1 2.4 select_select_fusion
  793.5 11.7 %while.13 = (s32[]{:T(128)}, f32[512,512]{1,0:T(8,128)}, s32[4,2]{0,1:T(2,128)S(1)}, f32[4,128,128]{2,1,0:T(8,128)S(1)}, s32[]{:T(128)}) while((s32[]{:T(128)}, f32[512,512]{1,0:T(8,128)}, s32[4,2]{0,1:T(2,128)S(1)}, f32[4,128,128]{2,1,0:T(8,128)S(1)}, s32[]{:T(128)}) %tuple.123), condition=%wide.while_cond.8.clone, body=%wide.while_body.8.clone.sunk | while | flops 2 | bytes 131189 | solution.py:68
  794.2 2.3 bitcast_dynamic-update-slice_fusion.5
  797.1 2.3 bitcast_dynamic-update-slice_fusion.5
  800.0 2.3 bitcast_dynamic-update-slice_fusion.5
  803.0 2.2 bitcast_dynamic-update-slice_fusion.5
  805.2 39.3 %custom-call.36 = f32[4,128,128]{1,2,0:T(8,128)S(1)} custom-call(f32[4,128,128]{2,1,0:T(8,128)S(1)} %get-tuple-element.118), custom_call_target="InvertDiagBlocksLowerTriangular" | custom-call | tf_op jit(solution)/shard_map/jit(_cho_solve)/triangular_solve | solution.py:68
  854.9 5.0 convert_subtract_fusion
  860.0 9.2 fusion.8
  869.3 25.8 %convolution_subtract_fusion = f32[1280,2560]{0,1:T(8,128)} fusion(f32[1280,2560]{0,1:T(8,128)S(1)} %bitcast.119, f32[512,2560]{1,0:T(8,128)S(1)} %fusion.8, f32[1280,512]{0,1:T(8,128)S(1)} %constant_dynamic-update-slice_fusion.8, s32[1280]{0:T(1024)S(1)} %broadcast_add_fusion), kind=kOutput, calls=%fused_computation.4 | convolution fusion | flops 20137902080 | bytes 34083840 | tf_op jit(solution)/shard_map/dot_general | solution.py:95
  895.1 2.8 constant_dynamic-update-slice_fusion.21
  897.9 1.6 fusion.66
  899.5 1.7 constant_dynamic-update-slice_fusion.20
  901.2 1.6 fusion.45
  902.8 13.9 %copy.13 = f32[1280,2560]{1,0:T(8,128)} copy(f32[1280,2560]{0,1:T(8,128)} %fusion.45) | data formatting | bytes 26214400 | tf_op jit(solution)/shard_map/scatter | solution.py:110
  (158 shorter events, 64.9 us)
Async XLA Ops:
  6.5 97.7 %all-reduce.16.cloned.1.call-start = ((), (), s32[]{:S(2)}) async-start(), calls=%async_computation.3 | async-start | bytes 5242880 | tf_op jit(solution)/shard_map/psum | solution.py:13
  23.1 221.0 %all-reduce.12.cloned.1.call-start = ((), (), s32[]{:S(2)}) async-start(), calls=%async_computation.1 | async-start | bytes 12582912 | tf_op jit(solution)/shard_map/psum | solution.py:13
  104.2 2.4 copy-start.8
  104.2 2.4 copy-start.7
  107.8 438.5 %all-reduce.14.cloned.1.call-start = ((), (), s32[]{:S(2)}) async-start(), calls=%async_computation.2 | async-start | bytes 5242880 | tf_op jit(solution)/shard_map/psum | solution.py:13
  255.2 1.0 copy-start.4
  411.9 5.3 copy-start.2
  415.1 22.6 %slice-start = ((s8[13107200]{0:T(1024)(128)(4,1)}), s8[4194304]{0:T(1024)(128)(4,1)S(1)}, s32[]{:S(2)}) async-start(s8[13107200]{0:T(1024)(128)(4,1)} %bitcast.116), calls=%async_computation.4 | async-start | bytes 8388608
  420.4 8.2 copy-start.12
  420.9 16.9 %slice-start.1 = ((s8[13107200]{0:T(1024)(128)(4,1)}), s8[4194304]{0:T(1024)(128)(4,1)S(1)}, s32[]{:S(2)}) async-start(s8[13107200]{0:T(1024)(128)(4,1)} %bitcast.116), calls=%async_computation.5 | async-start | bytes 8388608
  421.9 6.7 copy-start.9
  421.9 6.7 copy-start.10
  421.9 6.6 copy-start.11
  422.3 15.5 %slice-start.2 = ((s8[13107200]{0:T(1024)(128)(4,1)}), s8[4194304]{0:T(1024)(128)(4,1)S(1)}, s32[]{:S(2)}) async-start(s8[13107200]{0:T(1024)(128)(4,1)} %bitcast.116), calls=%async_computation.6 | async-start | bytes 8388608
  428.6 9.2 slice-start.3
  467.7 1.7 copy-start
  467.7 218.4 %all-reduce.10.cloned.1.call-start = ((), (), s32[]{:S(2)}) async-start(), calls=%async_computation | async-start | bytes 12582912 | tf_op jit(solution)/shard_map/psum | solution.py:13
  546.3 2.4 copy-start.6
  546.3 2.4 copy-start.5
  697.4 1.0 copy-start.3
  844.5 5.3 copy-start.1
  847.8 21.4 %slice-start.4 = ((s8[13107200]{0:T(1024)(128)(4,1)}), s8[4194304]{0:T(1024)(128)(4,1)S(1)}, s32[]{:S(2)}) async-start(s8[13107200]{0:T(1024)(128)(4,1)} %bitcast.118), calls=%async_computation.8 | async-start | bytes 8388608
  853.0 7.0 copy-start.16
  853.5 15.7 %slice-start.5 = ((s8[13107200]{0:T(1024)(128)(4,1)}), s8[4194304]{0:T(1024)(128)(4,1)S(1)}, s32[]{:S(2)}) async-start(s8[13107200]{0:T(1024)(128)(4,1)} %bitcast.118), calls=%async_computation.9 | async-start | bytes 8388608
  854.5 5.4 copy-start.13
  854.5 5.4 copy-start.14
  854.5 5.4 copy-start.15
  854.9 14.3 %slice-start.6 = ((s8[13107200]{0:T(1024)(128)(4,1)}), s8[4194304]{0:T(1024)(128)(4,1)S(1)}, s32[]{:S(2)}) async-start(s8[13107200]{0:T(1024)(128)(4,1)} %bitcast.118), calls=%async_computation.10 | async-start | bytes 8388608
  860.0 9.2 %slice-start.7 = ((s8[13107200]{0:T(1024)(128)(4,1)}), s8[524288]{0:T(1024)(128)(4,1)S(1)}, s32[]{:S(2)}) async-start(s8[13107200]{0:T(1024)(128)(4,1)} %bitcast.118), calls=%async_computation.11 | async-start | bytes 1048576
Sparse Core Ops, SparseCore 0:
  23.2 80.9 all-reduce.15
  107.9 136.1 all-reduce.11
  467.9 78.3 all-reduce.13
  550.0 136.1 all-reduce.9
where the time goes:
time: 935 us; the launch traced here: 924 us
  waiting for transfers between devices  413 us (44%)
  other arithmetic  289 us (31%)
  matrix products  121 us (13%)
  local copies, waits for them, and re-layouts  80.7 us (9%)
  between operations  19.2 us (2%)
    psum x4, waiting for transfers between devices, broadcast(): return lax.psum(kept, axis)  413 us
    another operation x29, other arithmetic, per_device(): lower = jnp.linalg.cholesky(pivot_block)  172 us
    another operation x5, other arithmetic, per_device(): prepare_inverse = jax.scipy.linalg.cho_solve((lower, True), identity)  83.3 us
    dot_general x2, matrix products, per_device(): jnp.dot(reduced, scaled, precision=lax.Precision.HIGHEST, preferred_eleme...  52.1 us
    unnamed x63, local copies, waits for them, and re-layouts  32.7 us
    another operation x27, local copies, waits for them, and re-layouts, per_device(): prepare_inverse = jax.scipy.linalg.cho_solve((lower, True), identity)  23.3 us
    another operation x28, matrix products, per_device(): prepare_inverse = jax.scipy.linalg.cho_solve((lower, True), identity)  20.5 us
  transfers between devices with their start and end apart: 4, of which 4 were waited for; matrix products, arithmetic and copies ran while one was open for 2% of the time, Pallas kernels for 0%

commit v1 on v0

--- a/solution.py
+++ b/solution.py
@@ -10,7 +10,7 @@
 
 def broadcast(value, axis, source):
     kept = jnp.where(lax.axis_index(axis) == source, value, 0).astype(value.dtype)
-    return lax.psum(kept, axis)
+    return jnp.sum(lax.all_gather(kept, axis), axis=0)
 
 
 def per_device(factor):

time: 935 us -> 1470 us (1.57)
  waiting for transfers between devices: 413 us -> 924 us
  other arithmetic: 289 us -> 356 us
  local copies, waits for them, and re-layouts: 80.7 us -> 42.2 us
    all_gather x0 -> x24, waiting for transfers between devices: none -> 914 us  [broadcast(): return jnp.sum(lax.all_gather(kept, axis), axis=0)]
    psum x4 -> x0, waiting for transfers between devices: 413 us -> none  [broadcast(): return lax.psum(kept, axis)]
    reduce_sum x0 -> x24, other arithmetic: none -> 83.7 us  [broadcast(): return jnp.sum(lax.all_gather(kept, axis), axis=0)]
    unnamed x63 -> x64, local copies, waits for them, and re-layouts: 32.7 us -> 13.7 us
  transfers between devices with their start and end apart: 4 -> 24, of which waited for: 4 -> 21; matrix products, arithmetic and copies ran while one was open for 2% -> 29% of each run, Pallas kernels for 0% -> 0%
where the time goes in v1:
time: 1470 us; the launch traced here: 1460 us
  waiting for transfers between devices  924 us (63%)
  other arithmetic  356 us (24%)
  matrix products  121 us (8%)
  local copies, waits for them, and re-layouts  42.2 us (3%)
  between operations  20.2 us (1%)
    all_gather x24, waiting for transfers between devices, broadcast(): return jnp.sum(lax.all_gather(kept, axis), axis=0)  914 us
    another operation x29, other arithmetic, per_device(): lower = jnp.linalg.cholesky(pivot_block)  164 us
    reduce_sum x24, other arithmetic, broadcast(): return jnp.sum(lax.all_gather(kept, axis), axis=0)  83.7 us
    another operation x5, other arithmetic, per_device(): prepare_inverse = jax.scipy.linalg.cho_solve((lower, True), identity)  81.9 us
    dot_general x2, matrix products, per_device(): jnp.dot(reduced, scaled, precision=lax.Precision.HIGHEST, preferred_eleme...  51.8 us
  transfers between devices with their start and end apart: 24, of which 21 were waited for; matrix products, arithmetic and copies ran while one was open for 29% of the time, Pallas kernels for 0%

profile of v1, /device:TPU:0, one launch (start us, length us, event | category | flops | bytes accessed | tf_op | source)
XLA Modules:
  0.0 1464.3 jit_solution(11056793224778936984)
XLA Ops:
  11.3 40.3 %all-gather.49.cloned.1.call-done = f32[5120,128]{1,0:T(8,128)} async-done(((f32[1280,128]{1,0:T(8,128)}), f32[5120,128]{1,0:T(8,128)}) %all-gather.49.cloned.1.call-update) | async-done | bytes 2621456 | tf_op jit(solution)/shard_map/all_gather | solution.py:13
  53.5 39.4 %all-gather.51.cloned.1.call-done = f32[5120,128]{1,0:T(8,128)} async-done(((f32[1280,128]{1,0:T(8,128)}), f32[5120,128]{1,0:T(8,128)}) %all-gather.51.cloned.1.call-update) | async-done | bytes 2621456 | tf_op jit(solution)/shard_map/all_gather | solution.py:13
  94.9 39.4 %all-gather.53.cloned.1.call-done = f32[5120,128]{1,0:T(8,128)} async-done(((f32[1280,128]{1,0:T(8,128)}), f32[5120,128]{1,0:T(8,128)}) %all-gather.53.cloned.1.call-update) | async-done | bytes 2621456 | tf_op jit(solution)/shard_map/all_gather | solution.py:13
  136.3 39.3 %all-gather.55.cloned.1.call-done = f32[5120,128]{1,0:T(8,128)} async-done(((f32[1280,128]{1,0:T(8,128)}), f32[5120,128]{1,0:T(8,128)}) %all-gather.55.cloned.1.call-update) | async-done | bytes 2621456 | tf_op jit(solution)/shard_map/all_gather | solution.py:13
  180.9 3.8 slice_select_fusion.7
  187.5 20.6 %all-gather.57.cloned.1.call-done = f32[1024,512]{1,0:T(8,128)} async-done(((f32[128,512]{1,0:T(8,128)}), f32[1024,512]{1,0:T(8,128)}) %all-gather.57.cloned.1.call-update) | async-done | bytes 2097168 | tf_op jit(solution)/shard_map/all_gather | solution.py:13
  210.0 28.1 %all-gather.59.cloned.1.call-done = f32[1024,512]{1,0:T(8,128)} async-done(((f32[128,512]{1,0:T(8,128)}), f32[1024,512]{1,0:T(8,128)}) %all-gather.59.cloned.1.call-update) | async-done | bytes 2097168 | tf_op jit(solution)/shard_map/all_gather | solution.py:13
  240.1 28.2 %all-gather.61.cloned.1.call-done = f32[1024,512]{1,0:T(8,128)} async-done(((f32[128,512]{1,0:T(8,128)}), f32[1024,512]{1,0:T(8,128)}) %all-gather.61.cloned.1.call-update) | async-done | bytes 2097168 | tf_op jit(solution)/shard_map/all_gather | solution.py:13
  270.2 28.2 %all-gather.63.cloned.1.call-done = f32[1024,512]{1,0:T(8,128)} async-done(((f32[128,512]{1,0:T(8,128)}), f32[1024,512]{1,0:T(8,128)}) %all-gather.63.cloned.1.call-update) | async-done | bytes 2097168 | tf_op jit(solution)/shard_map/all_gather | solution.py:13
  307.9 11.7 cholesky.286
  319.7 9.8 custom-call.29
  332.7 12.1 cholesky.305
  344.8 9.8 custom-call.30
  357.8 13.2 cholesky.326
  373.0 11.3 custom-call.31
  386.5 11.9 cholesky.343
  406.3 14.4 while.12
  407.0 3.0 bitcast_dynamic-update-slice_fusion.4
  410.6 2.9 bitcast_dynamic-update-slice_fusion.4
  414.2 2.9 bitcast_dynamic-update-slice_fusion.4
  417.8 2.9 bitcast_dynamic-update-slice_fusion.4
  420.7 40.8 %custom-call.32 = f32[4,128,128]{1,2,0:T(8,128)} custom-call(f32[4,128,128]{2,1,0:T(8,128)} %get-tuple-element.117), custom_call_target="InvertDiagBlocksLowerTriangular" | custom-call | tf_op jit(solution)/shard_map/jit(_cho_solve)/triangular_solve | solution.py:68
  472.0 6.1 reduce_sum.224
  478.1 20.0 %all-gather.67.cloned.1.call-done = f32[1024,2560]{1,0:T(8,128)} async-done(((f32[128,2560]{1,0:T(8,128)}), f32[1024,2560]{1,0:T(8,128)}) %all-gather.67.cloned.1.call-update) | async-done | bytes 10485776 | tf_op jit(solution)/shard_map/all_gather | solution.py:13
  498.2 6.2 reduce_sum.225
  504.3 93.2 %all-gather.69.cloned.1.call-done = f32[1024,2560]{1,0:T(8,128)} async-done(((f32[128,2560]{1,0:T(8,128)}), f32[1024,2560]{1,0:T(8,128)}) %all-gather.69.cloned.1.call-update) | async-done | bytes 10485776 | tf_op jit(solution)/shard_map/all_gather | solution.py:13
  597.5 6.1 reduce_sum.226
  603.7 93.1 %all-gather.71.cloned.1.call-done = f32[1024,2560]{1,0:T(8,128)} async-done(((f32[128,2560]{1,0:T(8,128)}), f32[1024,2560]{1,0:T(8,128)}) %all-gather.71.cloned.1.call-update) | async-done | bytes 10485776 | tf_op jit(solution)/shard_map/all_gather | solution.py:13
  696.8 6.1 reduce_sum.227
  702.9 11.3 fusion
  714.2 5.1 broadcast_select_fusion.3
  721.1 36.2 %all-gather.73.cloned.1.call-done = f32[5120,128]{1,0:T(8,128)} async-done(((f32[1280,128]{1,0:T(8,128)}), f32[5120,128]{1,0:T(8,128)}) %all-gather.73.cloned.1.call-update) | async-done | bytes 2621456 | tf_op jit(solution)/shard_map/all_gather | solution.py:13
  757.3 2.8 reduce_sum.228
  760.1 38.4 %all-gather.75.cloned.1.call-done = f32[5120,128]{1,0:T(8,128)} async-done(((f32[1280,128]{1,0:T(8,128)}), f32[5120,128]{1,0:T(8,128)}) %all-gather.75.cloned.1.call-update) | async-done | bytes 2621456 | tf_op jit(solution)/shard_map/all_gather | solution.py:13
  801.3 38.5 %all-gather.77.cloned.1.call-done = f32[5120,128]{1,0:T(8,128)} async-done(((f32[1280,128]{1,0:T(8,128)}), f32[5120,128]{1,0:T(8,128)}) %all-gather.77.cloned.1.call-update) | async-done | bytes 2621456 | tf_op jit(solution)/shard_map/all_gather | solution.py:13
  839.8 2.8 reduce_sum.230
  842.6 38.4 %all-gather.79.cloned.1.call-done = f32[5120,128]{1,0:T(8,128)} async-done(((f32[1280,128]{1,0:T(8,128)}), f32[5120,128]{1,0:T(8,128)}) %all-gather.79.cloned.1.call-update) | async-done | bytes 2621456 | tf_op jit(solution)/shard_map/all_gather | solution.py:13
  881.0 2.8 reduce_sum.231
  888.8 7.4 convert_subtract_fusion.2
  896.2 26.0 %convolution_subtract_fusion.1 = f32[1280,2560]{1,0:T(8,128)S(1)} fusion(f32[1280,2560]{1,0:T(8,128)} %param.20, f32[512,2560]{1,0:T(8,128)} %copy-done.10, s32[1280]{0:T(1024)S(1)} %fusion.122, f32[1280,128]{1,0:T(8,128)} %copy-done.4, f32[1280,128]{1,0:T(8,128)S(1)} %copy-done.3, f32[1280,128]{1,0:T(8,128)S(1)} %reduce_sum.217, ...), kind=kOutput, calls=%fused_computation.5 | convolution fusion | flops 20139868160 | bytes 34083840 | tf_op jit(solution)/shard_map/dot_general | solution.py:95
  925.4 4.9 copy-done
  937.9 8.2 all-gather.85.cloned.1.call-done
  948.1 28.2 %all-gather.87.cloned.1.call-done = f32[1024,512]{1,0:T(8,128)} async-done(((f32[128,512]{1,0:T(8,128)}), f32[1024,512]{1,0:T(8,128)}) %all-gather.87.cloned.1.call-update) | async-done | bytes 2097168 | tf_op jit(solution)/shard_map/all_gather | solution.py:13
  978.2 28.1 %all-gather.81.cloned.1.call-done = f32[1024,512]{1,0:T(8,128)} async-done(((f32[128,512]{1,0:T(8,128)}), f32[1024,512]{1,0:T(8,128)}) %all-gather.81.cloned.1.call-update) | async-done | bytes 2097168 | tf_op jit(solution)/shard_map/all_gather | solution.py:13
  1010.7 11.7 cholesky.358
  1022.6 9.8 custom-call.33
  1033.0 12.1 cholesky.377
  1045.2 9.8 custom-call.34
  1055.7 11.7 cholesky.398
  1067.4 9.8 custom-call.35
  1077.8 11.9 cholesky.415
  1095.1 8.2 while.13
  1103.3 39.3 %custom-call.36 = f32[4,128,128]{1,2,0:T(8,128)S(1)} custom-call(f32[4,128,128]{2,1,0:T(8,128)S(1)} %get-tuple-element.118), custom_call_target="InvertDiagBlocksLowerTriangular" | custom-call | tf_op jit(solution)/shard_map/jit(_cho_solve)/triangular_solve | solution.py:68
  1152.6 6.1 convert_subtract_fusion
  1158.6 6.2 reduce_sum.236
  1164.8 41.9 %all-gather.91.cloned.1.call-done = f32[1024,2560]{1,0:T(8,128)} async-done(((f32[128,2560]{1,0:T(8,128)}), f32[1024,2560]{1,0:T(8,128)}) %all-gather.91.cloned.1.call-update) | async-done | bytes 10485776 | tf_op jit(solution)/shard_map/all_gather | solution.py:13
  1206.7 6.1 reduce_sum.237
  1212.9 93.2 %all-gather.93.cloned.1.call-done = f32[1024,2560]{1,0:T(8,128)} async-done(((f32[128,2560]{1,0:T(8,128)}), f32[1024,2560]{1,0:T(8,128)}) %all-gather.93.cloned.1.call-update) | async-done | bytes 10485776 | tf_op jit(solution)/shard_map/all_gather | solution.py:13
  1306.1 6.4 reduce_sum.238
  1312.4 92.9 %all-gather.95.cloned.1.call-done = f32[1024,2560]{1,0:T(8,128)} async-done(((f32[128,2560]{1,0:T(8,128)}), f32[1024,2560]{1,0:T(8,128)}) %all-gather.95.cloned.1.call-update) | async-done | bytes 10485776 | tf_op jit(solution)/shard_map/all_gather | solution.py:13
  1405.3 6.1 reduce_sum.239
  1411.5 10.8 fusion.8
  1422.3 25.8 %convolution_subtract_fusion = f32[1280,2560]{1,0:T(8,128)S(1)} fusion(f32[1280,2560]{1,0:T(8,128)} %copy-done, f32[512,2560]{1,0:T(8,128)S(1)} %fusion.8, s32[1280]{0:T(1024)S(1)} %broadcast_add_fusion, f32[1280,128]{1,0:T(8,128)S(1)} %copy-done.9, f32[1280,128]{1,0:T(8,128)S(1)} %copy-done.8, f32[1280,128]{1,0:T(8,128)S(1)} %copy-done.7, ...), kind=kOutput, calls=%fused_computation.4 | convolution fusion | flops 20139868160 | bytes 34083840 | tf_op jit(solution)/shard_map/dot_general | solution.py:95
  1450.7 4.9 copy-done.1
  (248 shorter events, 118.0 us)
Async XLA Ops:
  6.5 45.0 %all-gather.49.cloned.1.call-start = ((), (), s32[]{:S(2)}) async-start(), calls=%async_computation | async-start | bytes 3276800 | tf_op jit(solution)/shard_map/all_gather | solution.py:13
  9.2 83.8 %all-gather.51.cloned.1.call-start = ((), (), s32[]{:S(2)}) async-start(), calls=%async_computation.1 | async-start | bytes 3276800 | tf_op jit(solution)/shard_map/all_gather | solution.py:13
  9.9 124.4 %all-gather.53.cloned.1.call-start = ((), (), s32[]{:S(2)}) async-start(), calls=%async_computation.2 | async-start | bytes 3276800 | tf_op jit(solution)/shard_map/all_gather | solution.py:13
  10.7 164.9 %all-gather.55.cloned.1.call-start = ((), (), s32[]{:S(2)}) async-start(), calls=%async_computation.3 | async-start | bytes 3276800 | tf_op jit(solution)/shard_map/all_gather | solution.py:13
  11.2 196.8 %all-gather.57.cloned.1.call-start = ((), (), s32[]{:S(2)}) async-start(), calls=%async_computation.4 | async-start | bytes 2359296 | tf_op jit(solution)/shard_map/all_gather | solution.py:13
  136.3 41.4 %copy-start.2 = (f32[1280,128]{1,0:T(8,128)}, f32[1280,128]{1,0:T(8,128)S(1)}, u32[]{:S(2)}) copy-start(f32[1280,128]{1,0:T(8,128)S(1)} %reduce_sum.218) | copy-start | bytes 1966084
  177.5 1.2 copy-start.4
  178.8 59.3 %all-gather.59.cloned.1.call-start = ((), (), s32[]{:S(2)}) async-start(), calls=%async_computation.5 | async-start | bytes 2359296 | tf_op jit(solution)/shard_map/all_gather | solution.py:13
  179.3 88.9 %all-gather.61.cloned.1.call-start = ((), (), s32[]{:S(2)}) async-start(), calls=%async_computation.6 | async-start | bytes 2359296 | tf_op jit(solution)/shard_map/all_gather | solution.py:13
  180.1 118.4 %all-gather.63.cloned.1.call-start = ((), (), s32[]{:S(2)}) async-start(), calls=%async_computation.7 | async-start | bytes 2359296 | tf_op jit(solution)/shard_map/all_gather | solution.py:13
  180.8 291.2 %all-gather.65.cloned.1.call-start = ((), (), s32[]{:S(2)}) async-start(), calls=%async_computation.8 | async-start | bytes 11796480 | tf_op jit(solution)/shard_map/all_gather | solution.py:13
  184.7 313.4 %all-gather.67.cloned.1.call-start = ((), (), s32[]{:S(2)}) async-start(), calls=%async_computation.9 | async-start | bytes 11796480 | tf_op jit(solution)/shard_map/all_gather | solution.py:13
  185.3 412.2 %all-gather.69.cloned.1.call-start = ((), (), s32[]{:S(2)}) async-start(), calls=%async_computation.10 | async-start | bytes 11796480 | tf_op jit(solution)/shard_map/all_gather | solution.py:13
  186.1 510.7 %all-gather.71.cloned.1.call-start = ((), (), s32[]{:S(2)}) async-start(), calls=%async_computation.11 | async-start | bytes 11796480 | tf_op jit(solution)/shard_map/all_gather | solution.py:13
  186.6 570.7 %all-gather.73.cloned.1.call-start = ((), (), s32[]{:S(2)}) async-start(), calls=%async_computation.12 | async-start | bytes 3276800 | tf_op jit(solution)/shard_map/all_gather | solution.py:13
  210.0 92.1 %copy-start.19 = (f32[128,512]{0,1:T(8,128)}, f32[128,512]{0,1:T(8,128)S(1)}, u32[]{:S(2)}) copy-start(f32[128,512]{0,1:T(8,128)S(1)} %copy.4) | copy-start | bytes 786436
  240.1 62.0 %copy-start.20 = (f32[128,512]{0,1:T(8,128)}, f32[128,512]{0,1:T(8,128)S(1)}, u32[]{:S(2)}) copy-start(f32[128,512]{0,1:T(8,128)S(1)} %copy.5) | copy-start | bytes 786436
  270.2 31.9 %copy-start.22 = (f32[128,512]{0,1:T(8,128)}, f32[128,512]{0,1:T(8,128)S(1)}, u32[]{:S(2)}) copy-start(f32[128,512]{0,1:T(8,128)S(1)} %copy.6) | copy-start | bytes 786436
  302.1 0.7 copy-start.24
  306.9 1.0 copy-start.17
  332.1 0.7 copy-start.30
  420.7 46.4 %copy-start.12 = (f32[512,512]{1,0:T(8,128)S(1)}, f32[512,512]{1,0:T(8,128)}, u32[]{:S(2)}) copy-start(f32[512,512]{1,0:T(8,128)} %get-tuple-element.334) | copy-start | bytes 3145732
  461.5 5.2 copy-start.26
  468.6 2.3 copy-start.13
  469.4 1.5 copy-start.18
  470.2 0.7 copy-start.27
  696.8 6.1 copy-start.14
  702.9 11.3 copy-start.3
  702.9 11.3 copy-start.5
  714.2 5.1 copy-start.10
  719.3 79.2 %all-gather.75.cloned.1.call-start = ((), (), s32[]{:S(2)}) async-start(), calls=%async_computation.13 | async-start | bytes 3276800 | tf_op jit(solution)/shard_map/all_gather | solution.py:13
  719.9 119.9 %all-gather.77.cloned.1.call-start = ((), (), s32[]{:S(2)}) async-start(), calls=%async_computation.14 | async-start | bytes 3276800 | tf_op jit(solution)/shard_map/all_gather | solution.py:13
  720.5 160.5 %all-gather.79.cloned.1.call-start = ((), (), s32[]{:S(2)}) async-start(), calls=%async_computation.15 | async-start | bytes 3276800 | tf_op jit(solution)/shard_map/all_gather | solution.py:13
  721.1 214.9 %all-gather.83.cloned.1.call-start = ((), (), s32[]{:S(2)}) async-start(), calls=%async_computation.17 | async-start | bytes 2359296 | tf_op jit(solution)/shard_map/all_gather | solution.py:13
  886.7 59.4 %all-gather.85.cloned.1.call-start = ((), (), s32[]{:S(2)}) async-start(), calls=%async_computation.18 | async-start | bytes 2359296 | tf_op jit(solution)/shard_map/all_gather | solution.py:13
  887.3 89.0 %all-gather.87.cloned.1.call-start = ((), (), s32[]{:S(2)}) async-start(), calls=%async_computation.19 | async-start | bytes 2359296 | tf_op jit(solution)/shard_map/all_gather | solution.py:13
  888.1 118.2 %all-gather.81.cloned.1.call-start = ((), (), s32[]{:S(2)}) async-start(), calls=%async_computation.16 | async-start | bytes 2359296 | tf_op jit(solution)/shard_map/all_gather | solution.py:13
  896.2 262.5 %all-gather.89.cloned.1.call-start = ((), (), s32[]{:S(2)}) async-start(), calls=%async_computation.20 | async-start | bytes 11796480 | tf_op jit(solution)/shard_map/all_gather | solution.py:13
  896.2 26.0 %copy-start.16 = (f32[1280,512]{1,0:T(8,128)S(1)}, f32[1280,512]{1,0:T(8,128)}, u32[]{:S(2)}) copy-start(f32[1280,512]{1,0:T(8,128)} %convert_subtract_fusion.2) | copy-start | bytes 7864324
  925.4 5.0 copy-start
  933.0 273.8 %all-gather.91.cloned.1.call-start = ((), (), s32[]{:S(2)}) async-start(), calls=%async_computation.21 | async-start | bytes 11796480 | tf_op jit(solution)/shard_map/all_gather | solution.py:13
  933.7 372.3 %all-gather.93.cloned.1.call-start = ((), (), s32[]{:S(2)}) async-start(), calls=%async_computation.22 | async-start | bytes 11796480 | tf_op jit(solution)/shard_map/all_gather | solution.py:13
  934.5 470.8 %all-gather.95.cloned.1.call-start = ((), (), s32[]{:S(2)}) async-start(), calls=%async_computation.23 | async-start | bytes 11796480 | tf_op jit(solution)/shard_map/all_gather | solution.py:13
  948.1 60.2 %copy-start.21 = (f32[128,512]{0,1:T(8,128)}, f32[128,512]{0,1:T(8,128)S(1)}, u32[]{:S(2)}) copy-start(f32[128,512]{0,1:T(8,128)S(1)} %copy.11) | copy-start | bytes 786436
  978.2 30.0 %copy-start.23 = (f32[128,512]{0,1:T(8,128)}, f32[128,512]{0,1:T(8,128)S(1)}, u32[]{:S(2)}) copy-start(f32[128,512]{0,1:T(8,128)S(1)} %copy.12) | copy-start | bytes 786436
  1008.3 0.7 copy-start.25
  1103.3 42.1 %copy-start.11 = (f32[512,512]{1,0:T(8,128)}, f32[512,512]{1,0:T(8,128)S(1)}, u32[]{:S(2)}) copy-start(f32[512,512]{1,0:T(8,128)S(1)} %get-tuple-element.333) | copy-start | bytes 3145732
  1146.2 6.4 copy-start.6
  1146.2 6.4 copy-start.7
  1146.2 6.4 copy-start.8
  1146.2 6.4 copy-start.9
  1149.7 2.1 copy-start.28
  1151.8 0.7 copy-start.31
  1405.3 6.1 copy-start.29
  1422.3 25.8 %copy-start.15 = (f32[1280,512]{1,0:T(8,128)S(1)}, f32[1280,512]{1,0:T(8,128)}, u32[]{:S(2)}) copy-start(f32[1280,512]{1,0:T(8,128)} %convert_subtract_fusion) | copy-start | bytes 7864324
  1450.7 5.0 copy-start.1
Sparse Core Ops, SparseCore 0:
  9.3 42.2 all-gather.48
  53.4 39.4 all-gather.50
  94.8 39.4 all-gather.52
  136.0 39.4 all-gather.54
  178.9 29.1 all-gather.56
  209.5 28.5 all-gather.58
  239.7 28.5 all-gather.60
  269.9 28.5 all-gather.62
  300.1 98.8 all-gather.64
  400.4 97.6 all-gather.66
  499.8 97.6 all-gather.68
  599.0 97.6 all-gather.70
  719.5 37.8 all-gather.72
  759.0 39.4 all-gather.74
  800.3 39.4 all-gather.76
  841.5 39.4 all-gather.78
  886.9 29.1 all-gather.82
  917.5 28.5 all-gather.84
  947.7 28.5 all-gather.86
  977.7 28.5 all-gather.80
  1008.0 98.9 all-gather.88
  1108.5 98.1 all-gather.90
  1208.4 97.6 all-gather.92
  1307.6 97.6 all-gather.94
